TPU v7x, 256 devices: a whole 4x4x8 slice. The times are simulated.
256 devices in a mesh: scen: 16 (over z_lo, y, core), tm: 16 (over z_hi, x).
Axes of the slice: x: 4, y: 4, z: 8 (z_hi: 4, z_lo: 2; z = z_hi * 2 + z_lo), core: 2. Of those that a mesh axis runs over, the one named last changes fastest.
Arguments:
- cotangent: float32 [64, 336, 2048], P('scen', 'tm'), may hold values from -6 to 6
- blocks: bfloat16 [16, 6, 128, 128], P('tm'), may hold values from -0.21875 to 0.21875
- zone_links: int32 [16, 6], replicated, may hold values from 0 to 15, as said below
- step_size: float32 [2048], replicated, may hold values from 0.3 to 1
- coupling: bfloat16 [16, 336, 336], P('tm'), may hold values from -0.3125 to 0.3125
- ramp_band: int32 [16], P('tm'), may hold values from 42 to 336, as said below
- candidates: int32 [2048], P('scen'), may hold values from 0 to 2047, as said below
Outputs:
- initial_adjoint: float32 [64, 336, 2048], P('scen', 'tm')
- siting_gradient: float32 [336, 2048], P('tm', 'scen')
Inputs may be any that keep to these rules, and one draw needn't show every extreme that they name: zone_links[z, 0] = z, and the 6 entries of a row are distinct zones. `ramp_band`: at least one zone has reach 336. `candidates`: the entries of block m of 128 consecutive entries are distinct buses in m * (128) to (m + 1) * 128 - 1.
All inputs are finite; a program needn't handle non-finite values.
Results may differ from a plain program's by a relative error of at most 0.0029.
Values may be sent and summed in bfloat16 or wider, within the bound.
No kernel may reach another device: no remote copies, remote signals or barrier semaphores. Data moves between devices by JAX's collectives and lax.ppermute only.
A program may use at most 64 MiB of HBM per device.

v0:
```python
import jax
import jax.numpy as jnp
from jax import lax
from jax.experimental import pallas as pl
from jax.experimental.pallas import tpu as pltpu
from jax.sharding import Mesh
from jax.sharding import PartitionSpec as P


SCEN = ("z_lo", "y", "core")
TM = ("z_hi", "x")
F32, BF16 = jnp.float32, jnp.bfloat16
VMEM_LIMIT = 48 * 1024 * 1024
SM = pl.BlockSpec(memory_space=pltpu.SMEM)
ANY = pl.BlockSpec(memory_space=pl.ANY)
VM = pl.BlockSpec()
SLOT = 96
NEXT = 88
NT = (((1,), (1,)), ((), ()))


def call(body, outs, specs, scratch=()):
    return pl.pallas_call(
        body,
        out_shape=outs,
        in_specs=specs,
        scratch_shapes=list(scratch),
        compiler_params=pltpu.CompilerParams(vmem_limit_bytes=VMEM_LIMIT),
    )


def strip_body(place, blocks, sent):
    count, width = sent.shape[1], blocks.shape[1]
    pick = (
        lax.broadcasted_iota(jnp.int32, (count, width), 1)
        == lax.broadcasted_iota(jnp.int32, (count, width), 0) + place[0] * count
    ).astype(F32).astype(BF16)
    own = lax.dot_general(pick, blocks[...], NT, preferred_element_type=F32).astype(BF16)
    for zone in range(sent.shape[0]):
        sent[zone] = own


def scenario_sum(rows, zone, hours, scens):
    total = rows[zone, pl.ds(0, hours, stride=scens), :]
    for scen in range(1, scens):
        total = total + rows[zone, pl.ds(scen, hours, stride=scens), :]
    return total


def scale_body(cot, step, scaled, rows):
    hours, scens, _ = cot.shape
    zones, _, width = scaled.shape
    for hour in range(hours):
        rows[scens * hour : scens * (hour + 1), :] = cot[hour] * step[...]
    for zone in range(zones):
        scaled[zone] = rows[:, width * zone : width * (zone + 1)].astype(BF16)


def strip_network_body(place, links, own, other, *rest):
    near = own.shape[1]
    size = (len(rest) - 3) // 2
    panels, outs, (gathered, weights, sems) = rest[:size], rest[size : 2 * size], rest[2 * size :]
    zones, count, width = gathered.shape[0], panels[0].shape[1], gathered.shape[2]
    copies = [
        pltpu.make_async_copy(panel, gathered.at[:, pl.ds(SLOT * n, count), :], sems.at[n])
        for n, panel in enumerate(panels)
    ]
    for copy in copies:
        copy.start()
    mine = pl.multiple_of(place[1] * near, 16)
    theirs = pl.multiple_of((1 - place[1]) * near, 16)
    weights[...] = jnp.zeros_like(weights)
    for zone in range(zones):
        base = 2 * near * zone
        for k in range(links.shape[1]):
            lanes = slice(width * k, width * (k + 1))
            weights[links[zone, k], pl.ds(base + mine, near), :] = own[zone, :, lanes]
            weights[links[zone, k], pl.ds(base + theirs, near), :] = other[zone, :, lanes]
    for copy in copies:
        copy.wait()
    panel = jnp.concatenate([gathered[zone] for zone in range(zones)], axis=1)
    step = 256
    for first in range(0, weights.shape[1], step):
        block = jnp.concatenate([weights[zone, first : first + step, :] for zone in range(zones)], axis=1)
        total = lax.dot_general(panel, block, NT, preferred_element_type=F32)
        for n in range(size):
            outs[n][:, first : first + step] = total[SLOT * n : SLOT * n + count].astype(BF16)


def masked_of(band, coupling):
    total = coupling.shape[0]
    spread = jnp.abs(
        lax.broadcasted_iota(jnp.int32, (total, total), 0)
        - lax.broadcasted_iota(jnp.int32, (total, total), 1)
    )
    return jnp.where(spread <= band[0], coupling[...].astype(F32), 0.0).astype(BF16)


def apply_temporal(band, coupling, rows, scens):
    total, width = coupling.shape[0], rows.shape[1]
    hours = jnp.concatenate(
        [rows[pl.ds(scen, total, stride=scens), :].astype(BF16) for scen in range(scens)], axis=1
    )
    result = lax.dot_general(
        masked_of(band, coupling), hours, (((0,), (0,)), ((), ())), preferred_element_type=F32
    )
    parts = [result[:, width * scen : width * (scen + 1)] for scen in range(scens)]
    for scen in range(scens):
        rows[pl.ds(scen, total, stride=scens), :] = parts[scen]
    return sum(parts[1:], parts[0])


def first_temporal_body(place, band, got, coupling, *rest):
    size = len(rest) - 5
    strips, (out, network, summed, rows, stack) = rest[:size], rest[size:]
    zones, count, width = got.shape
    scens = zones * count // coupling.shape[0]
    for zone in range(zones):
        rows[count * zone : count * (zone + 1), :] = got[zone].astype(F32)
    summed[...] = apply_temporal(band, coupling, rows, scens)
    for zone in range(zones):
        out[zone, 0:count, :] = rows[count * zone : count * (zone + 1), :].astype(BF16)
    for n in range(size):
        stack[lax.rem(place[0] + size - n, size)] = strips[n][...].astype(F32)
    wide = width // size
    lane = lax.broadcasted_iota(jnp.int32, (count, width), 1) // wide
    for zone in range(zones):
        first = width * (zone * wide // width)
        at = zone * wide % width // wide
        total = None
        for n in range(size):
            part = stack[n, :, first : first + width]
            if n != at:
                part = pltpu.roll(part, (n - at) % size * wide, 1)
            total = part if total is None else jnp.where(lane == n, part, total)
        value = total.astype(BF16)
        network[zone] = value
        out[zone, NEXT : NEXT + count, :] = value


def second_temporal_body(place, band, got, sent, back, coupling, step, out, rows):
    zones, count, _ = got.shape
    scens = zones * count // coupling.shape[0]
    own = step[pl.ds(place[3], 1), :]
    for zone in range(zones):
        both = sent[zone, 0:count, :].astype(F32) + back[zone, NEXT : NEXT + count, :].astype(F32)
        rows[count * zone : count * (zone + 1), :] = got[zone].astype(F32) - own * both
    apply_temporal(band, coupling, rows, scens)
    for zone in range(zones):
        out[zone] = rows[count * zone : count * (zone + 1), :].astype(BF16)


def sums_body(place, cot, network, summed, steps, *rest):
    outs, rows = rest[:-1], rest[-1]
    hours, scens, _ = cot.shape
    _, _, width = network.shape
    size = len(outs)
    part = outs[0].shape[1] // 2
    own = steps[pl.ds(place[3], 1), :]
    for d, out in enumerate(outs):
        y = lax.rem(place[2] + d, size)
        for n in range(4):
            zone = (n // 2) * (2 * size) + 2 * y + n % 2
            lanes = pl.ds(pl.multiple_of(zone * width, width), width)
            rows[n + 4 * d] = network[zone].astype(F32)
            total = 2.0 * jnp.sum(cot[:, :, lanes], axis=1) - scenario_sum(rows, n + 4 * d, hours, scens)
            out[n, 0:hours, :] = total * steps[pl.ds(zone, 1), :]
            out[n, hours:part, :] = jnp.zeros((part - hours, width), F32)
            out[n, part : part + hours, :] = -summed[zone] * own
            out[n, part + hours :, :] = jnp.zeros((part - hours, width), F32)


def network_body(place, links, cot, step, network, back, *rest):
    parts, (out, weights, rows, scaled, sems) = rest[:-5], rest[-5:]
    zones, near = out.shape[0], parts[0].shape[1]
    hours, scens, _ = cot.shape
    count, width = out.shape[1], out.shape[2]
    half = len(parts) // 2
    copies = []
    for n, part in enumerate(parts):
        core = place[1] if n < half else 1 - place[1]
        y = lax.rem(place[2] + (n % half), half)
        first = pl.multiple_of((y * 2 + core) * near, 16)
        copy = pltpu.make_async_copy(part, weights.at[:, pl.ds(first, near), :], sems.at[n])
        copy.start()
        copies.append(copy)
    for hour in range(hours):
        rows[scens * hour : scens * (hour + 1), :] = cot[hour]
    for zone in range(zones):
        lanes = slice(width * zone, width * (zone + 1))
        value = rows[:, lanes] - network[zone].astype(F32) - back[zone, 0:count, :].astype(F32)
        scaled[zone] = (value * step[:, lanes]).astype(BF16)
        out[zone] = value
    for copy in copies:
        copy.wait()
    for zone in range(zones):
        picked = jnp.concatenate([scaled[links[zone, k]] for k in range(links.shape[1])], axis=1)
        out[zone] = out[zone] - lax.dot_general(picked, weights[zone], NT, preferred_element_type=F32)


def finish_body(base, temporal, out):
    hours, scens, _ = out.shape
    zones, _, width = temporal.shape
    for zone in range(zones):
        value = base[zone] - temporal[zone].astype(F32)
        for hour in range(hours):
            out[hour, :, width * zone : width * (zone + 1)] = value[scens * hour : scens * (hour + 1)]


def siting_body(factor, place, kept, turned, columns, out):
    hours, width = out.shape
    wanted = columns[...] - place[4] * width
    pick = (lax.broadcasted_iota(jnp.int32, (width, width), 0) == wanted).astype(F32)
    total = (kept[...] + turned[...]) * factor
    moved = jnp.dot(total, pick, preferred_element_type=F32, precision=lax.Precision.HIGHEST)
    out[...] = moved[0:hours]


def ring(size, shift):
    return [(k, (k + shift) % size) for k in range(size)]


def exchange(array):
    return lax.all_to_all(array, TM, 0, 0, tiled=True)


def per_device(cotangent, blocks, zone_links, step_size, coupling, ramp_band, candidates):
    scens, hours, buses = cotangent.shape
    zones, width = zone_links.shape[0], blocks.shape[3]
    count, depth = hours * scens, blocks.shape[1] * width
    z_lo, y, core = (lax.axis_index(name) for name in SCEN)
    size_y = lax.axis_size("y")
    near = width // (2 * size_y)
    swap = [(0, 1), (1, 0)]
    place = jnp.stack([2 * y + core, core, y, lax.axis_index(TM), lax.axis_index(SCEN), z_lo]).astype(jnp.int32)
    cot = jnp.transpose(cotangent, (1, 0, 2))
    step = step_size.reshape(1, buses)
    sds = jax.ShapeDtypeStruct
    panel = sds((zones, count, width), BF16)
    wide_panel = sds((zones, count, width), F32)
    row_scratch = pltpu.VMEM((zones * count, width), F32)

    strips = call(strip_body, sds((zones, near, depth), BF16), [SM, VM])(
        place, blocks.reshape(depth, width)
    )
    own = exchange(strips)
    scaled0 = call(scale_body, panel, [VM, VM], [pltpu.VMEM((count, buses), F32)])(cot, step)
    panels = [scaled0] + [lax.ppermute(scaled0, "y", ring(size_y, -d)) for d in range(1, size_y)]
    other = lax.ppermute(own, "core", swap)
    got = exchange(scaled0)

    flat = sds((count, zones * width // size_y), BF16)
    made = call(
        strip_network_body,
        [flat] * size_y,
        [SM, SM, VM, VM] + [ANY] * size_y,
        [
            pltpu.VMEM((zones, SLOT * size_y, width), BF16),
            pltpu.VMEM((zones, zones * width // size_y, width), BF16),
            pltpu.SemaphoreType.DMA((size_y,)),
        ],
    )(place, zone_links, own, other, *panels)
    home = [made[0]] + [lax.ppermute(made[d], "y", ring(size_y, d)) for d in range(1, size_y)]

    sent, network0, summed = call(
        first_temporal_body,
        (sds((zones, NEXT + count, width), BF16), panel, sds((coupling.shape[1], width), F32)),
        [SM, SM, VM, VM] + [VM] * size_y,
        [row_scratch, pltpu.VMEM((size_y, count, zones * width // size_y), F32)],
    )(place[2:3], ramp_band, got, coupling[0], *home)
    back = exchange(sent)

    near_parts = [own] + [lax.ppermute(own, "y", ring(size_y, -d)) for d in range(1, size_y)]
    far_parts = [other] + [lax.ppermute(part, "core", swap) for part in near_parts[1:]]
    parts = near_parts + far_parts

    temporal1 = call(second_temporal_body, panel, [SM, SM] + [VM] * 5, [row_scratch])(
        place, ramp_band, got, sent, back, coupling[0], step_size.reshape(zones, width)
    )
    returned = exchange(temporal1)
    split = call(
        sums_body,
        [sds((4, 48, width), F32)] * size_y,
        [SM] + [VM] * 4,
        [pltpu.VMEM((zones, count, width), F32)],
    )(place, cot, network0, summed.reshape(zones, hours, width), step_size.reshape(zones, width))
    total = split[0]
    for d in range(1, size_y):
        total = total + lax.ppermute(split[d], "y", ring(size_y, d))
    total = total.reshape(2, 2, 48, width)
    total = total[:, core] + lax.ppermute(total[:, 1 - core], "core", swap)
    away = lax.ppermute(total[1 - z_lo], "z_lo", swap)
    total = total[z_lo] + away
    turned = lax.ppermute(
        total[24:], SCEN + TM, [(m * zones + z, z * zones + m) for m in range(zones) for z in range(zones)]
    )
    factor = 1.0 / (scens * lax.axis_size(SCEN))
    siting = call(
        lambda *refs: siting_body(factor, *refs), sds((hours, width), F32), [SM, VM, VM, VM]
    )(place, total[:24], turned, candidates.reshape(1, width))

    base = call(
        network_body,
        wide_panel,
        [SM, SM] + [VM] * 4 + [ANY] * len(parts),
        [
            pltpu.VMEM((zones, width, depth), BF16),
            pltpu.VMEM((count, buses), F32),
            pltpu.VMEM((zones, count, width), BF16),
            pltpu.SemaphoreType.DMA((len(parts),)),
        ],
    )(place, zone_links, cot, step, network0, back, *parts)
    out = call(finish_body, sds((hours, scens, buses), F32), [VM] * 2)(base, returned)
    return jnp.transpose(out, (1, 0, 2)), siting


def solution(mesh):
    fine = Mesh(mesh.devices.reshape(2, 4, 2, 4, 4), SCEN + TM)
    placed = (
        P(SCEN, TM, None),
        P(TM, None, None, None),
        P(),
        P(),
        P(TM, None, None),
        P(TM),
        P(SCEN),
    )
    return jax.shard_map(
        per_device,
        mesh=fine,
        in_specs=placed,
        out_specs=(P(SCEN, TM, None), P(TM, SCEN)),
        check_vma=False,
    )
```

profile of v0, /device:TPU:24, one launch (start us, length us, event | category | flops | bytes accessed | tf_op | source)
XLA Modules:
  0.0 135.2 jit_solution(6806063057891282584)
XLA Ops:
  0.6 0.1 stack.27.place.refs_0_
  0.7 0.9 copy-done.4
  1.7 1.5 %shard_map.87 = bf16[16,16,768]{2,1,0:T(8,128)(2,1)} custom-call(s32[6]{0:T(128)S(1)} %stack.27.place.refs_0_, bf16[768,128]{1,0:T(8,128)(2,1)S(1)} %bitcast.27), custom_call_target="tpu_custom_call" | custom-call | tf_op jit(solution)/shard_map/pallas_call | solution.py:243
  3.1 11.2 %all-to-all-start.1 = ((bf16[16,16,768]{2,1,0:T(8,128)(2,1)}), bf16[16,16,768]{2,1,0:T(8,128)(2,1)S(1)}, u32[]{:S(2)}, u32[]{:S(2)}) async-start(bf16[16,16,768]{2,1,0:T(8,128)(2,1)} %shard_map.87), calls=%async_computation.1 | async-start | bytes 786432 | tf_op jit(solution)/shard_map/all_to_all | solution.py:224
  14.3 0.0 copy-done
  14.3 0.0 copy-done.5
  14.3 0.9 shard_map.86.rest_0_
  15.2 13.8 %all-to-all-done.1.own.rest_0_ = bf16[16,16,768]{2,1,0:T(8,128)(2,1)S(1)} async-done(((bf16[16,16,768]{2,1,0:T(8,128)(2,1)}), bf16[16,16,768]{2,1,0:T(8,128)(2,1)S(1)}, u32[]{:S(2)}, u32[]{:S(2)}) %all-to-all-start.1) | async-done | bytes 393248 | tf_op jit(solution)/shard_map/all_to_all | solution.py:224
  29.0 4.3 %all-to-all-start = ((bf16[16,84,128]{2,1,0:T(8,128)(2,1)}), bf16[16,84,128]{2,1,0:T(8,128)(2,1)S(1)}, u32[]{:S(2)}, u32[]{:S(2)}) async-start(bf16[16,84,128]{2,1,0:T(8,128)(2,1)} %shard_map.86.rest_0_), calls=%async_computation | async-start | bytes 720896 | tf_op jit(solution)/shard_map/all_to_all | solution.py:224
  33.2 0.1 collective-permute-start
  33.4 0.8 collective-permute-start.1
  34.2 0.9 collective-permute-start.2
  35.1 2.2 %collective-permute-start.3 = (bf16[16,84,128]{2,1,0:T(8,128)(2,1)}, bf16[16,84,128]{2,1,0:T(8,128)(2,1)S(1)}, u32[]{:S(2)}, u32[]{:S(2)}) collective-permute-start(bf16[16,84,128]{2,1,0:T(8,128)(2,1)} %shard_map.86.rest_0_), channel_id=1, source_target_pairs={{0,32},{32,64},{64,96},{96,0},{1,33},{33,65},{65,97},{97,1},{2,34}... | collective-permute-start | bytes 1032200 | tf_op jit(solution)/shard_map/ppermute | solution.py:248
  37.3 0.0 copy-done.9
  37.3 0.1 copy.12.links
  37.4 15.9 %collective-permute-done.1.rest_1_ = bf16[16,84,128]{2,1,0:T(8,128)(2,1)S(1)} collective-permute-done((bf16[16,84,128]{2,1,0:T(8,128)(2,1)}, bf16[16,84,128]{2,1,0:T(8,128)(2,1)S(1)}, u32[]{:S(2)}, u32[]{:S(2)}) %collective-permute-start.1) | collective-permute-done | bytes 344096 | tf_op jit(solution)/shard_map/ppermute | solution.py:248
  53.3 0.0 collective-permute-done.2.rest_2_
  53.3 0.6 collective-permute-done.3.rest_3_
  53.9 0.0 collective-permute-done.other.rest_4_
  53.9 3.3 %shard_map.88 = (bf16[84,512]{1,0:T(8,128)(2,1)S(1)}, bf16[84,512]{1,0:T(8,128)(2,1)}, bf16[84,512]{1,0:T(8,128)(2,1)S(1)}, bf16[84,512]{1,0:T(8,128)(2,1)S(1)}) custom-call(s32[6]{0:T(128)S(1)} %stack.27.place.refs_0_, s32[16,6]{1,0:T(8,128)S(1)} %copy.12.links, bf16[16,16,768]{2,1,0:T(8,128)(2,1)S(1)} %all-to-all-done.1.own.rest_0_, ...), custom_call_target="tpu_custom_call" | custom-call | tf_op jit(solution)/shard_map/pallas_call | solution.py:253
  57.2 2.7 %collective-permute-start.4 = (bf16[84,512]{1,0:T(8,128)(2,1)}, bf16[84,512]{1,0:T(8,128)(2,1)S(1)}, u32[]{:S(2)}, u32[]{:S(2)}) collective-permute-start(bf16[84,512]{1,0:T(8,128)(2,1)} %get-tuple-element.14), channel_id=1, source_target_pairs={{0,32},{32,64},{64,96},{96,0},{1,33},{33,65},{65,97},{97,1},{2,34}... | collective-permute-start | bytes 258056 | tf_op jit(solution)/shard_map/ppermute | solution.py:263
  59.9 0.0 collective-permute-start.5
  60.0 0.9 collective-permute-start.6
  61.6 0.0 all-to-all-done.got
  61.6 2.7 %collective-permute-done.4.rest_1_ = bf16[84,512]{1,0:T(8,128)(2,1)S(1)} collective-permute-done((bf16[84,512]{1,0:T(8,128)(2,1)}, bf16[84,512]{1,0:T(8,128)(2,1)S(1)}, u32[]{:S(2)}, u32[]{:S(2)}) %collective-permute-start.4) | collective-permute-done | bytes 86048 | tf_op jit(solution)/shard_map/ppermute | solution.py:263
  64.3 2.4 %collective-permute-done.5.rest_2_ = bf16[84,512]{1,0:T(8,128)(2,1)S(1)} collective-permute-done((bf16[84,512]{1,0:T(8,128)(2,1)S(1)}, bf16[84,512]{1,0:T(8,128)(2,1)S(1)}, u32[]{:S(2)}, u32[]{:S(2)}) %collective-permute-start.5) | collective-permute-done | bytes 86048 | tf_op jit(solution)/shard_map/ppermute | solution.py:263
  66.7 0.7 collective-permute-done.6.rest_3_
  67.3 1.6 %shard_map.89 = (bf16[16,172,128]{2,1,0:T(8,128)(2,1)}, bf16[16,84,128]{2,1,0:T(8,128)(2,1)S(1)}, f32[336,128]{1,0:T(8,128)S(1)}) custom-call(s32[1]{0:T(128)} %bitcast.2.place, s32[1]{0:T(128)S(6)} %copy.13.band, bf16[16,84,128]{2,1,0:T(8,128)(2,1)S(1)} %all-to-all-done.got, bf16[336,336]{1,0:T(8,128)(2,1)S(1)} %bitcast.25, ...), custom_call_target="tpu_custom_call" | custom-call | tf_op jit(solution)/shard_map/pallas_call | solution.py:265
  69.0 9.5 %all-to-all-start.2 = ((bf16[16,172,128]{2,1,0:T(8,128)(2,1)}), bf16[16,172,128]{2,1,0:T(8,128)(2,1)S(1)}, u32[]{:S(2)}, u32[]{:S(2)}) async-start(bf16[16,172,128]{2,1,0:T(8,128)(2,1)} %get-tuple-element.18.sent), calls=%async_computation.2 | async-start | bytes 1441792 | tf_op jit(solution)/shard_map/all_to_all | solution.py:224
  78.5 1.7 %shard_map.93 = (f32[4,48,128]{2,1,0:T(8,128)S(1)}, f32[4,48,128]{2,1,0:T(8,128)}, f32[4,48,128]{2,1,0:T(8,128)}, f32[4,48,128]{2,1,0:T(8,128)}) custom-call(s32[6]{0:T(128)S(1)} %stack.27.place.refs_0_, f32[21,4,2048]{2,1,0:T(4,128)S(1)} %bitcast.23, bf16[16,84,128]{2,1,0:T(8,128)(2,1)S(1)} %get-tuple-element.17.network, ...), custom_call_target="tpu_custom_call" | custom-call | tf_op jit(solution)/shard_map/pallas_call | solution.py:281
  80.2 0.9 collective-permute-start.13
  81.1 0.3 collective-permute-start.14
  81.3 1.1 collective-permute-start.15
  82.5 3.2 %collective-permute-done.13 = f32[4,48,128]{2,1,0:T(8,128)S(1)} collective-permute-done((f32[4,48,128]{2,1,0:T(8,128)}, f32[4,48,128]{2,1,0:T(8,128)S(1)}, u32[]{:S(2)}, u32[]{:S(2)}) %collective-permute-start.13) | collective-permute-done | bytes 98336 | tf_op jit(solution)/shard_map/ppermute | solution.py:289
  85.6 2.6 %collective-permute-done.14 = f32[4,48,128]{2,1,0:T(8,128)S(1)} collective-permute-done((f32[4,48,128]{2,1,0:T(8,128)}, f32[4,48,128]{2,1,0:T(8,128)S(1)}, u32[]{:S(2)}, u32[]{:S(2)}) %collective-permute-start.14) | collective-permute-done | bytes 98336 | tf_op jit(solution)/shard_map/ppermute | solution.py:289
  88.2 0.4 collective-permute-done.15
  88.7 0.1 collective-permute-start.16
  88.8 0.1 collective-permute-start.7
  88.8 2.6 %collective-permute-start.8 = (bf16[16,16,768]{2,1,0:T(8,128)(2,1)S(1)}, bf16[16,16,768]{2,1,0:T(8,128)(2,1)}, u32[]{:S(2)}, u32[]{:S(2)}) collective-permute-start(bf16[16,16,768]{2,1,0:T(8,128)(2,1)S(1)} %all-to-all-done.1.own.rest_0_), channel_id=1, source_target_pairs={{0,64},{32,96},{64,0},{96,32},{1,65},{33,97},{65,1},{97,33},{2,66}... | collective-permute-start | bytes 1179656 | tf_op jit(solution)/shard_map/ppermute | solution.py:273
  91.5 0.8 collective-permute-start.9
  92.3 4.7 %all-to-all-done.2.back = bf16[16,172,128]{2,1,0:T(8,128)(2,1)S(1)} async-done(((bf16[16,172,128]{2,1,0:T(8,128)(2,1)}), bf16[16,172,128]{2,1,0:T(8,128)(2,1)S(1)}, u32[]{:S(2)}, u32[]{:S(2)}) %all-to-all-start.2) | async-done | bytes 704544 | tf_op jit(solution)/shard_map/all_to_all | solution.py:224
  97.0 2.4 %shard_map.91 = bf16[16,84,128]{2,1,0:T(8,128)(2,1)} custom-call(s32[6]{0:T(128)S(1)} %stack.27.place.refs_0_, s32[1]{0:T(128)S(6)} %copy.13.band, bf16[16,84,128]{2,1,0:T(8,128)(2,1)S(1)} %all-to-all-done.got, bf16[16,172,128]{2,1,0:T(8,128)(2,1)} %get-tuple-element.18.sent, bf16[16,172,128]{2,1,0:T(8,128)(2,1)S(1)} %all-to-all-done.2.back, ...), custom_call_target="tpu_custom_call" | custom-call | tf_op jit(solution)/shard_map/pallas_call | solution.py:277
  99.4 7.2 %all-to-all-start.3 = ((bf16[16,84,128]{2,1,0:T(8,128)(2,1)}), bf16[16,84,128]{2,1,0:T(8,128)(2,1)S(1)}, u32[]{:S(2)}, u32[]{:S(2)}) async-start(bf16[16,84,128]{2,1,0:T(8,128)(2,1)} %shard_map.91), calls=%async_computation.3 | async-start | bytes 720896 | tf_op jit(solution)/shard_map/all_to_all | solution.py:224
  106.6 0.0 collective-permute-done.16
  106.7 2.7 %collective-permute-start.17 = (f32[48,128]{1,0:T(8,128)S(1)}, f32[48,128]{1,0:T(8,128)S(1)}, u32[]{:S(2)}, u32[]{:S(2)}) collective-permute-start(f32[48,128]{1,0:T(8,128)S(1)} %dynamic-slice_bitcast_fusion.1), channel_id=1, source_target_pairs={{0,128},{128,0},{1,129},{129,1},{2,130},{130,2},{3,131},{131,3},{4... | collective-permute-start | bytes 73736 | tf_op jit(solution)/shard_map/ppermute | solution.py:292
  109.3 0.7 collective-permute-done.7.rest_1_
  110.0 0.0 collective-permute-start.10
  110.0 0.0 collective-permute-done.8.rest_2_
  110.0 0.5 collective-permute-start.11
  110.5 0.1 collective-permute-done.9.rest_3_
  110.6 0.0 collective-permute-start.12
  110.6 6.3 %collective-permute-done.17 = f32[48,128]{1,0:T(8,128)S(1)} collective-permute-done((f32[48,128]{1,0:T(8,128)S(1)}, f32[48,128]{1,0:T(8,128)S(1)}, u32[]{:S(2)}, u32[]{:S(2)}) %collective-permute-start.17) | collective-permute-done | bytes 24608 | tf_op jit(solution)/shard_map/ppermute | solution.py:292
  116.9 6.4 %collective-permute-start.18 = (f32[24,128]{1,0:T(8,128)S(1)}, f32[24,128]{1,0:T(8,128)S(1)}, u32[]{:S(2)}, u32[]{:S(2)}) collective-permute-start(f32[24,128]{1,0:T(8,128)S(1)} %get-tuple-element.24), channel_id=1, source_target_pairs={{0,0},{1,16},{2,32},{3,48},{4,64},{5,80},{6,96},{7,112},{8,128},{9... | collective-permute-start | bytes 36872 | tf_op jit(solution)/shard_map/ppermute | solution.py:294
  123.4 4.6 %collective-permute-done.18.refs_2_ = f32[24,128]{1,0:T(8,128)S(1)} collective-permute-done((f32[24,128]{1,0:T(8,128)S(1)}, f32[24,128]{1,0:T(8,128)S(1)}, u32[]{:S(2)}, u32[]{:S(2)}) %collective-permute-start.18) | collective-permute-done | bytes 12320 | tf_op jit(solution)/shard_map/ppermute | solution.py:294
  128.0 0.7 copy-done.8
  128.6 1.3 shard_map.94
  129.9 0.0 collective-permute-done.10.rest_5_
  129.9 0.0 collective-permute-done.11.rest_6_
  129.9 0.0 collective-permute-done.12.rest_7_
  129.9 0.0 copy-start.2
  130.0 1.0 copy-done.2
  130.9 3.2 %shard_map.90.base = f32[16,84,128]{2,1,0:T(8,128)S(1)} custom-call(s32[6]{0:T(128)S(1)} %stack.27.place.refs_0_, s32[16,6]{1,0:T(8,128)S(1)} %copy-done.7, f32[21,4,2048]{2,1,0:T(4,128)S(1)} %bitcast.24, f32[1,2048]{1,0:T(1,128)S(1)} %bitcast.31, bf16[16,84,128]{2,1,0:T(8,128)(2,1)S(1)} %copy-done.2, bf16[16,172,128]{2,1,0:T(8,128)(2,1)S(1)} %all-to-all-done.2.back, ...), custom_call_target="tpu_custom_call" | custom-call | tf_op jit(solution)/shard_map/pallas_call | solution.py:302
  134.2 0.0 all-to-all-done.3.temporal
  134.2 1.0 shard_map.92
  (20 shorter events, 0.1 us)
Async XLA Ops:
  0.7 0.9 copy-start.4
  1.7 12.7 %copy-start = (f32[4,21,2048]{2,0,1:T(4,128)S(1)}, f32[4,21,2048]{2,0,1:T(4,128)}, u32[]{:S(2)}) copy-start(f32[4,21,2048]{2,0,1:T(4,128)} %param.7) | copy-start | bytes 2064388
  3.1 11.2 %copy-start.5 = (f32[2048]{0:T(1024)S(1)}, f32[2048]{0:T(1024)}, u32[]{:S(2)}) copy-start(f32[2048]{0:T(1024)} %param.10) | copy-start | bytes 24580
  3.1 25.8 %all-to-all-start.1 = ((bf16[16,16,768]{2,1,0:T(8,128)(2,1)}), bf16[16,16,768]{2,1,0:T(8,128)(2,1)S(1)}, u32[]{:S(2)}, u32[]{:S(2)}) async-start(bf16[16,16,768]{2,1,0:T(8,128)(2,1)} %shard_map.87), calls=%async_computation.1 | async-start | bytes 786432 | tf_op jit(solution)/shard_map/all_to_all | solution.py:224
  15.2 22.1 %copy-start.9 = (s32[16,6]{0,1:T(8,128)S(1)}, s32[16,6]{0,1:T(8,128)}, u32[]{:S(2)}) copy-start(s32[16,6]{0,1:T(8,128)} %param.9) | copy-start | bytes 1156
  29.0 32.6 %all-to-all-start = ((bf16[16,84,128]{2,1,0:T(8,128)(2,1)}), bf16[16,84,128]{2,1,0:T(8,128)(2,1)S(1)}, u32[]{:S(2)}, u32[]{:S(2)}) async-start(bf16[16,84,128]{2,1,0:T(8,128)(2,1)} %shard_map.86.rest_0_), calls=%async_computation | async-start | bytes 720896 | tf_op jit(solution)/shard_map/all_to_all | solution.py:224
  33.2 20.7 %collective-permute-start = (bf16[16,16,768]{2,1,0:T(8,128)(2,1)S(1)}, bf16[16,16,768]{2,1,0:T(8,128)(2,1)S(1)}, u32[]{:S(2)}, u32[]{:S(2)}) collective-permute-start(bf16[16,16,768]{2,1,0:T(8,128)(2,1)S(1)} %all-to-all-done.1.own.rest_0_), channel_id=1, source_target_pairs={{0,16},{16,0},{1,17},{17,1},{2,18},{18,2},{3,19},{19,3},{4,20},{20... | collective-permute-start | bytes 1179656 | tf_op jit(solution)/shard_map/ppermute | solution.py:249
  33.4 20.0 %collective-permute-start.1 = (bf16[16,84,128]{2,1,0:T(8,128)(2,1)}, bf16[16,84,128]{2,1,0:T(8,128)(2,1)S(1)}, u32[]{:S(2)}, u32[]{:S(2)}) collective-permute-start(bf16[16,84,128]{2,1,0:T(8,128)(2,1)} %shard_map.86.rest_0_), channel_id=1, source_target_pairs={{0,96},{32,0},{64,32},{96,64},{1,97},{33,1},{65,33},{97,65},{2,98}... | collective-permute-start | bytes 1032200 | tf_op jit(solution)/shard_map/ppermute | solution.py:248
  34.2 19.1 %collective-permute-start.2 = (bf16[16,84,128]{2,1,0:T(8,128)(2,1)}, bf16[16,84,128]{2,1,0:T(8,128)(2,1)S(1)}, u32[]{:S(2)}, u32[]{:S(2)}) collective-permute-start(bf16[16,84,128]{2,1,0:T(8,128)(2,1)} %shard_map.86.rest_0_), channel_id=1, source_target_pairs={{0,64},{32,96},{64,0},{96,32},{1,65},{33,97},{65,1},{97,33},{2,66}... | collective-permute-start | bytes 1032200 | tf_op jit(solution)/shard_map/ppermute | solution.py:248
  35.1 18.8 %collective-permute-start.3 = (bf16[16,84,128]{2,1,0:T(8,128)(2,1)}, bf16[16,84,128]{2,1,0:T(8,128)(2,1)S(1)}, u32[]{:S(2)}, u32[]{:S(2)}) collective-permute-start(bf16[16,84,128]{2,1,0:T(8,128)(2,1)} %shard_map.86.rest_0_), channel_id=1, source_target_pairs={{0,32},{32,64},{64,96},{96,0},{1,33},{33,65},{65,97},{97,1},{2,34}... | collective-permute-start | bytes 1032200 | tf_op jit(solution)/shard_map/ppermute | solution.py:248
  37.4 19.8 %copy-start.6 = (s32[16,6]{1,0:T(8,128)}, s32[16,6]{1,0:T(8,128)S(1)}, u32[]{:S(2)}) copy-start(s32[16,6]{1,0:T(8,128)S(1)} %copy.12.links) | copy-start | bytes 1156
  37.4 30.0 %copy-start.3 = (bf16[1,336,336]{2,1,0:T(8,128)(2,1)S(1)}, bf16[1,336,336]{2,1,0:T(8,128)(2,1)}, u32[]{:S(2)}) copy-start(bf16[1,336,336]{2,1,0:T(8,128)(2,1)} %param.11) | copy-start | bytes 677380
  57.2 7.0 %collective-permute-start.4 = (bf16[84,512]{1,0:T(8,128)(2,1)}, bf16[84,512]{1,0:T(8,128)(2,1)S(1)}, u32[]{:S(2)}, u32[]{:S(2)}) collective-permute-start(bf16[84,512]{1,0:T(8,128)(2,1)} %get-tuple-element.14), channel_id=1, source_target_pairs={{0,32},{32,64},{64,96},{96,0},{1,33},{33,65},{65,97},{97,1},{2,34}... | collective-permute-start | bytes 258056 | tf_op jit(solution)/shard_map/ppermute | solution.py:263
  59.9 6.7 %collective-permute-start.5 = (bf16[84,512]{1,0:T(8,128)(2,1)S(1)}, bf16[84,512]{1,0:T(8,128)(2,1)S(1)}, u32[]{:S(2)}, u32[]{:S(2)}) collective-permute-start(bf16[84,512]{1,0:T(8,128)(2,1)S(1)} %get-tuple-element.15), channel_id=1, source_target_pairs={{0,64},{32,96},{64,0},{96,32},{1,65},{33,97},{65,1},{97,33},{2,66}... | collective-permute-start | bytes 258056 | tf_op jit(solution)/shard_map/ppermute | solution.py:263
  60.0 7.4 %collective-permute-start.6 = (bf16[84,512]{1,0:T(8,128)(2,1)S(1)}, bf16[84,512]{1,0:T(8,128)(2,1)S(1)}, u32[]{:S(2)}, u32[]{:S(2)}) collective-permute-start(bf16[84,512]{1,0:T(8,128)(2,1)S(1)} %get-tuple-element.16), channel_id=1, source_target_pairs={{0,96},{32,0},{64,32},{96,64},{1,97},{33,1},{65,33},{97,65},{2,98}... | collective-permute-start | bytes 258056 | tf_op jit(solution)/shard_map/ppermute | solution.py:263
  69.0 9.6 %copy-start.1 = (bf16[16,84,128]{2,1,0:T(8,128)(2,1)}, bf16[16,84,128]{2,1,0:T(8,128)(2,1)S(1)}, u32[]{:S(2)}) copy-start(bf16[16,84,128]{2,1,0:T(8,128)(2,1)S(1)} %get-tuple-element.17.network) | copy-start | bytes 1032196
  69.0 28.0 %all-to-all-start.2 = ((bf16[16,172,128]{2,1,0:T(8,128)(2,1)}), bf16[16,172,128]{2,1,0:T(8,128)(2,1)S(1)}, u32[]{:S(2)}, u32[]{:S(2)}) async-start(bf16[16,172,128]{2,1,0:T(8,128)(2,1)} %get-tuple-element.18.sent), calls=%async_computation.2 | async-start | bytes 1441792 | tf_op jit(solution)/shard_map/all_to_all | solution.py:224
  80.2 5.4 %collective-permute-start.13 = (f32[4,48,128]{2,1,0:T(8,128)}, f32[4,48,128]{2,1,0:T(8,128)S(1)}, u32[]{:S(2)}, u32[]{:S(2)}) collective-permute-start(f32[4,48,128]{2,1,0:T(8,128)} %get-tuple-element.21), channel_id=1, source_target_pairs={{0,32},{32,64},{64,96},{96,0},{1,33},{33,65},{65,97},{97,1},{2,34}... | collective-permute-start | bytes 294920 | tf_op jit(solution)/shard_map/ppermute | solution.py:289
  81.1 7.2 %collective-permute-start.14 = (f32[4,48,128]{2,1,0:T(8,128)}, f32[4,48,128]{2,1,0:T(8,128)S(1)}, u32[]{:S(2)}, u32[]{:S(2)}) collective-permute-start(f32[4,48,128]{2,1,0:T(8,128)} %get-tuple-element.22), channel_id=1, source_target_pairs={{0,64},{32,96},{64,0},{96,32},{1,65},{33,97},{65,1},{97,33},{2,66}... | collective-permute-start | bytes 294920 | tf_op jit(solution)/shard_map/ppermute | solution.py:289
  81.3 7.3 %collective-permute-start.15 = (f32[4,48,128]{2,1,0:T(8,128)}, f32[4,48,128]{2,1,0:T(8,128)S(1)}, u32[]{:S(2)}, u32[]{:S(2)}) collective-permute-start(f32[4,48,128]{2,1,0:T(8,128)} %get-tuple-element.23), channel_id=1, source_target_pairs={{0,96},{32,0},{64,32},{96,64},{1,97},{33,1},{65,33},{97,65},{2,98}... | collective-permute-start | bytes 294920 | tf_op jit(solution)/shard_map/ppermute | solution.py:289
  88.7 18.0 %collective-permute-start.16 = (f32[2,48,128]{2,1,0:T(8,128)S(1)}, f32[2,48,128]{2,1,0:T(8,128)S(1)}, u32[]{:S(2)}, u32[]{:S(2)}) collective-permute-start(f32[2,48,128]{2,1,0:T(8,128)S(1)} %dynamic-slice_bitcast_fusion), channel_id=1, source_target_pairs={{0,16},{16,0},{1,17},{17,1},{2,18},{18,2},{3,19},{19,3},{4,20},{20... | collective-permute-start | bytes 147464 | tf_op jit(solution)/shard_map/ppermute | solution.py:291
  88.8 21.3 %collective-permute-start.7 = (bf16[16,16,768]{2,1,0:T(8,128)(2,1)S(1)}, bf16[16,16,768]{2,1,0:T(8,128)(2,1)}, u32[]{:S(2)}, u32[]{:S(2)}) collective-permute-start(bf16[16,16,768]{2,1,0:T(8,128)(2,1)S(1)} %all-to-all-done.1.own.rest_0_), channel_id=1, source_target_pairs={{0,96},{32,0},{64,32},{96,64},{1,97},{33,1},{65,33},{97,65},{2,98}... | collective-permute-start | bytes 1179656 | tf_op jit(solution)/shard_map/ppermute | solution.py:273
  88.8 21.2 %collective-permute-start.8 = (bf16[16,16,768]{2,1,0:T(8,128)(2,1)S(1)}, bf16[16,16,768]{2,1,0:T(8,128)(2,1)}, u32[]{:S(2)}, u32[]{:S(2)}) collective-permute-start(bf16[16,16,768]{2,1,0:T(8,128)(2,1)S(1)} %all-to-all-done.1.own.rest_0_), channel_id=1, source_target_pairs={{0,64},{32,96},{64,0},{96,32},{1,65},{33,97},{65,1},{97,33},{2,66}... | collective-permute-start | bytes 1179656 | tf_op jit(solution)/shard_map/ppermute | solution.py:273
  91.5 19.2 %collective-permute-start.9 = (bf16[16,16,768]{2,1,0:T(8,128)(2,1)S(1)}, bf16[16,16,768]{2,1,0:T(8,128)(2,1)}, u32[]{:S(2)}, u32[]{:S(2)}) collective-permute-start(bf16[16,16,768]{2,1,0:T(8,128)(2,1)S(1)} %all-to-all-done.1.own.rest_0_), channel_id=1, source_target_pairs={{0,32},{32,64},{64,96},{96,0},{1,33},{33,65},{65,97},{97,1},{2,34}... | collective-permute-start | bytes 1179656 | tf_op jit(solution)/shard_map/ppermute | solution.py:273
  99.4 34.7 %all-to-all-start.3 = ((bf16[16,84,128]{2,1,0:T(8,128)(2,1)}), bf16[16,84,128]{2,1,0:T(8,128)(2,1)S(1)}, u32[]{:S(2)}, u32[]{:S(2)}) async-start(bf16[16,84,128]{2,1,0:T(8,128)(2,1)} %shard_map.91), calls=%async_computation.3 | async-start | bytes 720896 | tf_op jit(solution)/shard_map/all_to_all | solution.py:224
  106.7 10.2 %collective-permute-start.17 = (f32[48,128]{1,0:T(8,128)S(1)}, f32[48,128]{1,0:T(8,128)S(1)}, u32[]{:S(2)}, u32[]{:S(2)}) collective-permute-start(f32[48,128]{1,0:T(8,128)S(1)} %dynamic-slice_bitcast_fusion.1), channel_id=1, source_target_pairs={{0,128},{128,0},{1,129},{129,1},{2,130},{130,2},{3,131},{131,3},{4... | collective-permute-start | bytes 73736 | tf_op jit(solution)/shard_map/ppermute | solution.py:292
  110.0 19.9 %collective-permute-start.10 = (bf16[16,16,768]{2,1,0:T(8,128)(2,1)}, bf16[16,16,768]{2,1,0:T(8,128)(2,1)S(1)}, u32[]{:S(2)}, u32[]{:S(2)}) collective-permute-start(bf16[16,16,768]{2,1,0:T(8,128)(2,1)} %collective-permute-done.7.rest_1_), channel_id=1, source_target_pairs={{0,16},{16,0},{1,17},{17,1},{2,18},{18,2},{3,19},{19,3},{4,20},{20... | collective-permute-start | bytes 1179656 | tf_op jit(solution)/shard_map/ppermute | solution.py:274
  110.0 19.9 %collective-permute-start.11 = (bf16[16,16,768]{2,1,0:T(8,128)(2,1)}, bf16[16,16,768]{2,1,0:T(8,128)(2,1)S(1)}, u32[]{:S(2)}, u32[]{:S(2)}) collective-permute-start(bf16[16,16,768]{2,1,0:T(8,128)(2,1)} %collective-permute-done.8.rest_2_), channel_id=1, source_target_pairs={{0,16},{16,0},{1,17},{17,1},{2,18},{18,2},{3,19},{19,3},{4,20},{20... | collective-permute-start | bytes 1179656 | tf_op jit(solution)/shard_map/ppermute | solution.py:274
  110.6 19.3 %collective-permute-start.12 = (bf16[16,16,768]{2,1,0:T(8,128)(2,1)}, bf16[16,16,768]{2,1,0:T(8,128)(2,1)S(1)}, u32[]{:S(2)}, u32[]{:S(2)}) collective-permute-start(bf16[16,16,768]{2,1,0:T(8,128)(2,1)} %collective-permute-done.9.rest_3_), channel_id=1, source_target_pairs={{0,16},{16,0},{1,17},{17,1},{2,18},{18,2},{3,19},{19,3},{4,20},{20... | collective-permute-start | bytes 1179656 | tf_op jit(solution)/shard_map/ppermute | solution.py:274
  116.9 11.0 %collective-permute-start.18 = (f32[24,128]{1,0:T(8,128)S(1)}, f32[24,128]{1,0:T(8,128)S(1)}, u32[]{:S(2)}, u32[]{:S(2)}) collective-permute-start(f32[24,128]{1,0:T(8,128)S(1)} %get-tuple-element.24), channel_id=1, source_target_pairs={{0,0},{1,16},{2,32},{3,48},{4,64},{5,80},{6,96},{7,112},{8,128},{9... | collective-permute-start | bytes 36872 | tf_op jit(solution)/shard_map/ppermute | solution.py:294
  128.0 0.7 copy-start.8
  128.6 1.3 copy-start.7
  129.9 1.0 copy-start.2
where the time goes:
time: 136 us; the launch traced here: 135 us
  waiting for transfers between devices  58.6 us (43%)
  starting transfers between devices  55.3 us (41%)
  Pallas kernels  16.9 us (12%)
  local copies, waits for them, and re-layouts  2.81 us (2%)
  between operations  1.51 us (1%)
    all_to_all x4, starting transfers between devices, exchange(): return lax.all_to_all(array, TM, 0, 0, tiled=True)  32.2 us
    all_to_all x4, waiting for transfers between devices, exchange(): return lax.all_to_all(array, TM, 0, 0, tiled=True)  18.5 us
    ppermute x3, waiting for transfers between devices, per_device(): lax.ppermute(scaled0, 'y', ring(size_y, -d))  16.5 us
    ppermute x1, starting transfers between devices, per_device(): lax.ppermute(total[24:], SCEN + TM, [(m * zones + z, z * zones + m) for m...  6.41 us
    ppermute x1, waiting for transfers between devices, per_device(): away = lax.ppermute(total[1 - z_lo], 'z_lo', swap)  6.3 us
    ppermute x3, waiting for transfers between devices, per_device(): total = total + lax.ppermute(split[d], 'y', ring(size_y, d))  6.15 us
    ppermute x3, waiting for transfers between devices, per_device(): lax.ppermute(made[d], 'y', ring(size_y, d))  5.78 us
    ppermute x1, waiting for transfers between devices, per_device(): lax.ppermute(total[24:], SCEN + TM, [(m * zones + z, z * zones + m) for m...  4.58 us
  transfers between devices with their start and end apart: 23, of which 14 were waited for; matrix products, arithmetic and copies ran while one was open for 0% of the time, Pallas kernels for 9%

commit v1 on v0

--- a/solution.py
+++ b/solution.py
@@ -72,10 +72,10 @@
     weights[...] = jnp.zeros_like(weights)
     for zone in range(zones):
         base = 2 * near * zone
-        for k in range(links.shape[1]):
+        for k in range(links.shape[0]):
             lanes = slice(width * k, width * (k + 1))
-            weights[links[zone, k], pl.ds(base + mine, near), :] = own[zone, :, lanes]
-            weights[links[zone, k], pl.ds(base + theirs, near), :] = other[zone, :, lanes]
+            weights[links[k, zone], pl.ds(base + mine, near), :] = own[zone, :, lanes]
+            weights[links[k, zone], pl.ds(base + theirs, near), :] = other[zone, :, lanes]
     for copy in copies:
         copy.wait()
     panel = jnp.concatenate([gathered[zone] for zone in range(zones)], axis=1)
@@ -138,13 +138,19 @@
         out[zone, NEXT : NEXT + count, :] = value
 
 
-def second_temporal_body(place, band, got, sent, back, coupling, step, out, rows):
+def second_temporal_body(place, band, got, sent, back, coupling, step, out, rows, come, sem):
     zones, count, _ = got.shape
     scens = zones * count // coupling.shape[0]
+    copy = pltpu.make_async_copy(back.at[:, pl.ds(NEXT, count), :], come, sem)
+    copy.start()
     own = step[pl.ds(place[3], 1), :]
     for zone in range(zones):
-        both = sent[zone, 0:count, :].astype(F32) + back[zone, NEXT : NEXT + count, :].astype(F32)
-        rows[count * zone : count * (zone + 1), :] = got[zone].astype(F32) - own * both
+        value = got[zone].astype(F32) - own * sent[zone, 0:count, :].astype(F32)
+        rows[count * zone : count * (zone + 1), :] = value
+    copy.wait()
+    for zone in range(zones):
+        lines = slice(count * zone, count * (zone + 1))
+        rows[lines, :] = rows[lines, :] - own * come[zone].astype(F32)
     apply_temporal(band, coupling, rows, scens)
     for zone in range(zones):
         out[zone] = rows[count * zone : count * (zone + 1), :].astype(BF16)
@@ -194,7 +200,7 @@
     for copy in copies:
         copy.wait()
     for zone in range(zones):
-        picked = jnp.concatenate([scaled[links[zone, k]] for k in range(links.shape[1])], axis=1)
+        picked = jnp.concatenate([scaled[links[k, zone]] for k in range(links.shape[0])], axis=1)
         out[zone] = out[zone] - lax.dot_general(picked, weights[zone], NT, preferred_element_type=F32)
 
 
@@ -236,6 +242,7 @@
     cot = jnp.transpose(cotangent, (1, 0, 2))
     step = step_size.reshape(1, buses)
     sds = jax.ShapeDtypeStruct
+    links = zone_links.T
     panel = sds((zones, count, width), BF16)
     wide_panel = sds((zones, count, width), F32)
     row_scratch = pltpu.VMEM((zones * count, width), F32)
@@ -259,7 +266,7 @@
             pltpu.VMEM((zones, zones * width // size_y, width), BF16),
             pltpu.SemaphoreType.DMA((size_y,)),
         ],
-    )(place, zone_links, own, other, *panels)
+    )(place, links, own, other, *panels)
     home = [made[0]] + [lax.ppermute(made[d], "y", ring(size_y, d)) for d in range(1, size_y)]
 
     sent, network0, summed = call(
@@ -274,7 +281,12 @@
     far_parts = [other] + [lax.ppermute(part, "core", swap) for part in near_parts[1:]]
     parts = near_parts + far_parts
 
-    temporal1 = call(second_temporal_body, panel, [SM, SM] + [VM] * 5, [row_scratch])(
+    temporal1 = call(
+        second_temporal_body,
+        panel,
+        [SM, SM, VM, VM, ANY, VM, VM],
+        [row_scratch, pltpu.VMEM((zones, count, width), BF16), pltpu.SemaphoreType.DMA],
+    )(
         place, ramp_band, got, sent, back, coupling[0], step_size.reshape(zones, width)
     )
     returned = exchange(temporal1)
@@ -288,9 +300,13 @@
     for d in range(1, size_y):
         total = total + lax.ppermute(split[d], "y", ring(size_y, d))
     total = total.reshape(2, 2, 48, width)
-    total = total[:, core] + lax.ppermute(total[:, 1 - core], "core", swap)
-    away = lax.ppermute(total[1 - z_lo], "z_lo", swap)
-    total = total[z_lo] + away
+    mine = total[z_lo]
+    away = [
+        lax.ppermute(total[1 - z_lo, core], "z_lo", swap),
+        lax.ppermute(total[1 - z_lo, 1 - core], ("z_lo", "core"), [(n, 3 - n) for n in range(4)]),
+        lax.ppermute(mine[1 - core], "core", swap),
+    ]
+    total = mine[core] + away[0] + away[1] + away[2]
     turned = lax.ppermute(
         total[24:], SCEN + TM, [(m * zones + z, z * zones + m) for m in range(zones) for z in range(zones)]
     )
@@ -309,7 +325,7 @@
             pltpu.VMEM((zones, count, width), BF16),
             pltpu.SemaphoreType.DMA((len(parts),)),
         ],
-    )(place, zone_links, cot, step, network0, back, *parts)
+    )(place, links, cot, step, network0, back, *parts)
     out = call(finish_body, sds((hours, scens, buses), F32), [VM] * 2)(base, returned)
     return jnp.transpose(out, (1, 0, 2)), siting
 

time: 136 us -> 136 us (level)
  starting transfers between devices: 55.3 us -> 58.2 us
  waiting for transfers between devices: 58.6 us -> 56.2 us
    ppermute x3, waiting for transfers between devices: 6.15 us -> 0.01 us  [per_device(): total = total + lax.ppermute(split[d], 'y', ring(size_y, d))]
    all_to_all x4, waiting for transfers between devices: 18.5 us -> 21.8 us  [exchange(): return lax.all_to_all(array, TM, 0, 0, tiled=True)]
    ppermute x3, starting transfers between devices: 3.52 us -> 6.55 us  [per_device(): lax.ppermute(own, 'y', ring(size_y, -d))]
    ppermute x2 -> x3, waiting for transfers between devices: 6.3 us -> 6.79 us  [the longest x1 6.78 us: per_device(): lax.ppermute(total[1 - z_lo, core], 'z_lo', swap)]
    ppermute x2 -> x3, starting transfers between devices: 2.75 us -> 2.97 us  [the longest x1 2.75 us: per_device(): lax.ppermute(total[1 - z_lo, core], 'z_lo', swap)]
  transfers between devices with their start and end apart: 23 -> 24, of which waited for: 14 -> 9; matrix products, arithmetic and copies ran while one was open for 0% -> 0% of each run, Pallas kernels for 9% -> 9%
where the time goes in v1:
time: 136 us; the launch traced here: 135 us
  starting transfers between devices  58.2 us (43%)
  waiting for transfers between devices  56.2 us (41%)
  Pallas kernels  16.2 us (12%)
  local copies, waits for them, and re-layouts  2.71 us (2%)
  between operations  1.51 us (1%)
    all_to_all x4, starting transfers between devices, exchange(): return lax.all_to_all(array, TM, 0, 0, tiled=True)  32.2 us
    all_to_all x4, waiting for transfers between devices, exchange(): return lax.all_to_all(array, TM, 0, 0, tiled=True)  21.8 us
    ppermute x3, waiting for transfers between devices, per_device(): lax.ppermute(scaled0, 'y', ring(size_y, -d))  16.6 us
    ppermute x1, waiting for transfers between devices, per_device(): lax.ppermute(total[1 - z_lo, core], 'z_lo', swap)  6.78 us
    ppermute x3, starting transfers between devices, per_device(): lax.ppermute(own, 'y', ring(size_y, -d))  6.55 us
    ppermute x1, starting transfers between devices, per_device(): lax.ppermute(total[24:], SCEN + TM, [(m * zones + z, z * zones + m) for m...  5.99 us
    ppermute x3, waiting for transfers between devices, per_device(): lax.ppermute(made[d], 'y', ring(size_y, d))  5.79 us
    ppermute x1, waiting for transfers between devices, per_device(): lax.ppermute(total[24:], SCEN + TM, [(m * zones + z, z * zones + m) for m...  5.13 us
  transfers between devices with their start and end apart: 24, of which 9 were waited for; matrix products, arithmetic and copies ran while one was open for 0% of the time, Pallas kernels for 9%

profile of v1, /device:TPU:24, one launch (start us, length us, event | category | flops | bytes accessed | tf_op | source)
XLA Modules:
  0.0 134.8 jit_solution(9531591010554386113)
XLA Ops:
  0.6 0.1 stack.27.place.refs_0_
  0.7 0.9 copy-done.4
  1.7 1.5 %shard_map.87 = bf16[16,16,768]{2,1,0:T(8,128)(2,1)} custom-call(s32[6]{0:T(128)S(1)} %stack.27.place.refs_0_, bf16[768,128]{1,0:T(8,128)(2,1)S(1)} %bitcast.32), custom_call_target="tpu_custom_call" | custom-call | tf_op jit(solution)/shard_map/pallas_call | solution.py:250
  3.1 11.2 %all-to-all-start.1 = ((bf16[16,16,768]{2,1,0:T(8,128)(2,1)}), bf16[16,16,768]{2,1,0:T(8,128)(2,1)S(1)}, u32[]{:S(2)}, u32[]{:S(2)}) async-start(bf16[16,16,768]{2,1,0:T(8,128)(2,1)} %shard_map.87), calls=%async_computation.1 | async-start | bytes 786432 | tf_op jit(solution)/shard_map/all_to_all | solution.py:230
  14.3 0.0 copy-done
  14.3 0.9 shard_map.86.rest_0_
  15.2 13.8 %all-to-all-done.1.own.rest_0_ = bf16[16,16,768]{2,1,0:T(8,128)(2,1)S(1)} async-done(((bf16[16,16,768]{2,1,0:T(8,128)(2,1)}), bf16[16,16,768]{2,1,0:T(8,128)(2,1)S(1)}, u32[]{:S(2)}, u32[]{:S(2)}) %all-to-all-start.1) | async-done | bytes 393248 | tf_op jit(solution)/shard_map/all_to_all | solution.py:230
  29.0 4.4 %all-to-all-start = ((bf16[16,84,128]{2,1,0:T(8,128)(2,1)}), bf16[16,84,128]{2,1,0:T(8,128)(2,1)S(1)}, u32[]{:S(2)}, u32[]{:S(2)}) async-start(bf16[16,84,128]{2,1,0:T(8,128)(2,1)} %shard_map.86.rest_0_), calls=%async_computation | async-start | bytes 720896 | tf_op jit(solution)/shard_map/all_to_all | solution.py:230
  33.4 0.1 collective-permute-start
  33.5 0.8 collective-permute-start.1
  34.3 0.9 collective-permute-start.2
  35.2 2.2 %collective-permute-start.3 = (bf16[16,84,128]{2,1,0:T(8,128)(2,1)}, bf16[16,84,128]{2,1,0:T(8,128)(2,1)S(1)}, u32[]{:S(2)}, u32[]{:S(2)}) collective-permute-start(bf16[16,84,128]{2,1,0:T(8,128)(2,1)} %shard_map.86.rest_0_), channel_id=1, source_target_pairs={{0,32},{32,64},{64,96},{96,0},{1,33},{33,65},{65,97},{97,1},{2,34}... | collective-permute-start | bytes 1032200 | tf_op jit(solution)/shard_map/ppermute | solution.py:255
  37.4 16.0 %collective-permute-done.1.rest_1_ = bf16[16,84,128]{2,1,0:T(8,128)(2,1)S(1)} collective-permute-done((bf16[16,84,128]{2,1,0:T(8,128)(2,1)}, bf16[16,84,128]{2,1,0:T(8,128)(2,1)S(1)}, u32[]{:S(2)}, u32[]{:S(2)}) %collective-permute-start.1) | collective-permute-done | bytes 344096 | tf_op jit(solution)/shard_map/ppermute | solution.py:255
  53.4 0.0 collective-permute-done.2.rest_2_
  53.4 0.6 collective-permute-done.3.rest_3_
  54.1 0.0 collective-permute-done.other.rest_4_
  54.1 2.6 %shard_map.88 = (bf16[84,512]{1,0:T(8,128)(2,1)S(1)}, bf16[84,512]{1,0:T(8,128)(2,1)S(1)}, bf16[84,512]{1,0:T(8,128)(2,1)S(1)}, bf16[84,512]{1,0:T(8,128)(2,1)S(1)}) custom-call(s32[6]{0:T(128)S(1)} %stack.27.place.refs_0_, s32[6,16]{1,0:T(8,128)S(1)} %bitcast.37, bf16[16,16,768]{2,1,0:T(8,128)(2,1)S(1)} %all-to-all-done.1.own.rest_0_, ...), custom_call_target="tpu_custom_call" | custom-call | tf_op jit(solution)/shard_map/pallas_call | solution.py:260
  56.7 2.7 %collective-permute-start.4 = (bf16[84,512]{1,0:T(8,128)(2,1)S(1)}, bf16[84,512]{1,0:T(8,128)(2,1)S(1)}, u32[]{:S(2)}, u32[]{:S(2)}) collective-permute-start(bf16[84,512]{1,0:T(8,128)(2,1)S(1)} %get-tuple-element.14), channel_id=1, source_target_pairs={{0,32},{32,64},{64,96},{96,0},{1,33},{33,65},{65,97},{97,1},{2,34}... | collective-permute-start | bytes 258056 | tf_op jit(solution)/shard_map/ppermute | solution.py:270
  59.4 0.0 collective-permute-start.5
  59.5 0.9 collective-permute-start.6
  61.0 0.0 all-to-all-done.got
  61.0 2.4 %collective-permute-done.4.rest_1_ = bf16[84,512]{1,0:T(8,128)(2,1)S(1)} collective-permute-done((bf16[84,512]{1,0:T(8,128)(2,1)S(1)}, bf16[84,512]{1,0:T(8,128)(2,1)S(1)}, u32[]{:S(2)}, u32[]{:S(2)}) %collective-permute-start.4) | collective-permute-done | bytes 86048 | tf_op jit(solution)/shard_map/ppermute | solution.py:270
  63.4 2.7 %collective-permute-done.5.rest_2_ = bf16[84,512]{1,0:T(8,128)(2,1)S(1)} collective-permute-done((bf16[84,512]{1,0:T(8,128)(2,1)S(1)}, bf16[84,512]{1,0:T(8,128)(2,1)S(1)}, u32[]{:S(2)}, u32[]{:S(2)}) %collective-permute-start.5) | collective-permute-done | bytes 86048 | tf_op jit(solution)/shard_map/ppermute | solution.py:270
  66.2 0.7 collective-permute-done.6.rest_3_
  66.8 1.6 %shard_map.89 = (bf16[16,172,128]{2,1,0:T(8,128)(2,1)}, bf16[16,84,128]{2,1,0:T(8,128)(2,1)S(1)}, f32[336,128]{1,0:T(8,128)S(1)}) custom-call(s32[1]{0:T(128)} %bitcast.2.place, s32[1]{0:T(128)S(6)} %copy.9.band, bf16[16,84,128]{2,1,0:T(8,128)(2,1)S(1)} %all-to-all-done.got, bf16[336,336]{1,0:T(8,128)(2,1)S(1)} %bitcast.30, ...), custom_call_target="tpu_custom_call" | custom-call | tf_op jit(solution)/shard_map/pallas_call | solution.py:272
  68.4 9.5 %all-to-all-start.2 = ((bf16[16,172,128]{2,1,0:T(8,128)(2,1)}), bf16[16,172,128]{2,1,0:T(8,128)(2,1)S(1)}, u32[]{:S(2)}, u32[]{:S(2)}) async-start(bf16[16,172,128]{2,1,0:T(8,128)(2,1)} %get-tuple-element.18.sent), calls=%async_computation.2 | async-start | bytes 1441792 | tf_op jit(solution)/shard_map/all_to_all | solution.py:230
  78.0 0.0 copy-done.1
  78.0 1.7 %shard_map.93 = (f32[4,48,128]{2,1,0:T(8,128)S(1)}, f32[4,48,128]{2,1,0:T(8,128)S(1)}, f32[4,48,128]{2,1,0:T(8,128)}, f32[4,48,128]{2,1,0:T(8,128)}) custom-call(s32[6]{0:T(128)S(1)} %stack.27.place.refs_0_, f32[21,4,2048]{2,1,0:T(4,128)S(1)} %bitcast.28, bf16[16,84,128]{2,1,0:T(8,128)(2,1)S(1)} %get-tuple-element.17.network, ...), custom_call_target="tpu_custom_call" | custom-call | tf_op jit(solution)/shard_map/pallas_call | solution.py:293
  79.7 0.9 collective-permute-start.13
  80.5 0.3 collective-permute-start.14
  80.8 1.1 collective-permute-start.15
  81.9 2.1 %collective-permute-start.7 = (bf16[16,16,768]{2,1,0:T(8,128)(2,1)S(1)}, bf16[16,16,768]{2,1,0:T(8,128)(2,1)}, u32[]{:S(2)}, u32[]{:S(2)}) collective-permute-start(bf16[16,16,768]{2,1,0:T(8,128)(2,1)S(1)} %all-to-all-done.1.own.rest_0_), channel_id=1, source_target_pairs={{0,96},{32,0},{64,32},{96,64},{1,97},{33,1},{65,33},{97,65},{2,98}... | collective-permute-start | bytes 1179656 | tf_op jit(solution)/shard_map/ppermute | solution.py:280
  84.0 1.8 %collective-permute-start.8 = (bf16[16,16,768]{2,1,0:T(8,128)(2,1)S(1)}, bf16[16,16,768]{2,1,0:T(8,128)(2,1)}, u32[]{:S(2)}, u32[]{:S(2)}) collective-permute-start(bf16[16,16,768]{2,1,0:T(8,128)(2,1)S(1)} %all-to-all-done.1.own.rest_0_), channel_id=1, source_target_pairs={{0,64},{32,96},{64,0},{96,32},{1,65},{33,97},{65,1},{97,33},{2,66}... | collective-permute-start | bytes 1179656 | tf_op jit(solution)/shard_map/ppermute | solution.py:280
  85.8 0.0 collective-permute-done.13
  85.9 2.6 %collective-permute-start.9 = (bf16[16,16,768]{2,1,0:T(8,128)(2,1)S(1)}, bf16[16,16,768]{2,1,0:T(8,128)(2,1)}, u32[]{:S(2)}, u32[]{:S(2)}) collective-permute-start(bf16[16,16,768]{2,1,0:T(8,128)(2,1)S(1)} %all-to-all-done.1.own.rest_0_), channel_id=1, source_target_pairs={{0,32},{32,64},{64,96},{96,0},{1,33},{33,65},{65,97},{97,1},{2,34}... | collective-permute-start | bytes 1179656 | tf_op jit(solution)/shard_map/ppermute | solution.py:280
  88.5 8.0 %all-to-all-done.2.back = bf16[16,172,128]{2,1,0:T(8,128)(2,1)S(1)} async-done(((bf16[16,172,128]{2,1,0:T(8,128)(2,1)}), bf16[16,172,128]{2,1,0:T(8,128)(2,1)S(1)}, u32[]{:S(2)}, u32[]{:S(2)}) %all-to-all-start.2) | async-done | bytes 704544 | tf_op jit(solution)/shard_map/all_to_all | solution.py:230
  96.5 2.5 %shard_map.91 = bf16[16,84,128]{2,1,0:T(8,128)(2,1)} custom-call(s32[6]{0:T(128)S(1)} %stack.27.place.refs_0_, s32[1]{0:T(128)S(6)} %copy.9.band, bf16[16,84,128]{2,1,0:T(8,128)(2,1)S(1)} %all-to-all-done.got, bf16[16,172,128]{2,1,0:T(8,128)(2,1)} %get-tuple-element.18.sent, bf16[16,172,128]{2,1,0:T(8,128)(2,1)S(1)} %all-to-all-done.2.back, ...), custom_call_target="tpu_custom_call" | custom-call | tf_op jit(solution)/shard_map/pallas_call | solution.py:284
  99.0 7.1 %all-to-all-start.3 = ((bf16[16,84,128]{2,1,0:T(8,128)(2,1)}), bf16[16,84,128]{2,1,0:T(8,128)(2,1)S(1)}, u32[]{:S(2)}, u32[]{:S(2)}) async-start(bf16[16,84,128]{2,1,0:T(8,128)(2,1)} %shard_map.91), calls=%async_computation.3 | async-start | bytes 720896 | tf_op jit(solution)/shard_map/all_to_all | solution.py:230
  106.1 0.0 collective-permute-done.14
  106.1 0.0 collective-permute-done.15
  106.2 2.8 %collective-permute-start.16 = (f32[48,128]{1,0:T(8,128)S(1)}, f32[48,128]{1,0:T(8,128)S(1)}, u32[]{:S(2)}, u32[]{:S(2)}) collective-permute-start(f32[48,128]{1,0:T(8,128)S(1)} %get-tuple-element.24), channel_id=1, source_target_pairs={{0,128},{128,0},{1,129},{129,1},{2,130},{130,2},{3,131},{131,3},{4... | collective-permute-start | bytes 73736 | tf_op jit(solution)/shard_map/ppermute | solution.py:305
  108.9 0.0 collective-permute-start.17
  108.9 0.0 collective-permute-done.7.rest_1_
  108.9 0.2 collective-permute-start.18
  109.2 0.0 collective-permute-done.8.rest_2_
  109.2 0.3 collective-permute-start.10
  109.5 0.0 collective-permute-done.9.rest_3_
  109.5 0.2 collective-permute-start.11
  109.7 6.8 %collective-permute-done.16 = f32[48,128]{1,0:T(8,128)S(1)} collective-permute-done((f32[48,128]{1,0:T(8,128)S(1)}, f32[48,128]{1,0:T(8,128)S(1)}, u32[]{:S(2)}, u32[]{:S(2)}) %collective-permute-start.16) | collective-permute-done | bytes 24608 | tf_op jit(solution)/shard_map/ppermute | solution.py:305
  116.5 0.0 collective-permute-start.12
  116.5 0.0 collective-permute-done.17
  116.5 0.0 collective-permute-done.18
  116.5 6.0 %collective-permute-start.19 = (f32[24,128]{1,0:T(8,128)S(1)}, f32[24,128]{1,0:T(8,128)S(1)}, u32[]{:S(2)}, u32[]{:S(2)}) collective-permute-start(f32[24,128]{1,0:T(8,128)S(1)} %get-tuple-element.27), channel_id=1, source_target_pairs={{0,0},{1,16},{2,32},{3,48},{4,64},{5,80},{6,96},{7,112},{8,128},{9... | collective-permute-start | bytes 36872 | tf_op jit(solution)/shard_map/ppermute | solution.py:310
  122.5 5.1 %collective-permute-done.19.refs_2_ = f32[24,128]{1,0:T(8,128)S(1)} collective-permute-done((f32[24,128]{1,0:T(8,128)S(1)}, f32[24,128]{1,0:T(8,128)S(1)}, u32[]{:S(2)}, u32[]{:S(2)}) %collective-permute-start.19) | collective-permute-done | bytes 12320 | tf_op jit(solution)/shard_map/ppermute | solution.py:310
  127.6 0.7 copy-done.8
  128.3 1.3 shard_map.94
  129.6 0.0 collective-permute-done.10.rest_5_
  129.6 0.0 collective-permute-done.11.rest_6_
  129.6 0.0 collective-permute-done.12.rest_7_
  129.6 0.0 copy-start.2
  129.6 1.0 copy-done.2
  130.6 3.2 %shard_map.90.base = f32[16,84,128]{2,1,0:T(8,128)S(1)} custom-call(s32[6]{0:T(128)S(1)} %stack.27.place.refs_0_, s32[6,16]{1,0:T(8,128)S(1)} %bitcast.38, f32[21,4,2048]{2,1,0:T(4,128)S(1)} %bitcast.29, f32[1,2048]{1,0:T(1,128)S(1)} %bitcast.36, bf16[16,84,128]{2,1,0:T(8,128)(2,1)S(1)} %copy-done.2, bf16[16,172,128]{2,1,0:T(8,128)(2,1)S(1)} %all-to-all-done.2.back, ...), custom_call_target="tpu_custom_call" | custom-call | tf_op jit(solution)/shard_map/pallas_call | solution.py:318
  133.8 0.0 all-to-all-done.3.temporal
  133.8 1.0 shard_map.92
  (17 shorter events, 0.1 us)
Async XLA Ops:
  0.7 0.9 copy-start.4
  1.7 12.7 %copy-start = (f32[4,21,2048]{2,0,1:T(4,128)S(1)}, f32[4,21,2048]{2,0,1:T(4,128)}, u32[]{:S(2)}) copy-start(f32[4,21,2048]{2,0,1:T(4,128)} %param.7) | copy-start | bytes 2064388
  3.1 11.2 %copy-start.5 = (f32[2048]{0:T(1024)S(1)}, f32[2048]{0:T(1024)}, u32[]{:S(2)}) copy-start(f32[2048]{0:T(1024)} %param.10) | copy-start | bytes 24580
  3.1 25.8 %all-to-all-start.1 = ((bf16[16,16,768]{2,1,0:T(8,128)(2,1)}), bf16[16,16,768]{2,1,0:T(8,128)(2,1)S(1)}, u32[]{:S(2)}, u32[]{:S(2)}) async-start(bf16[16,16,768]{2,1,0:T(8,128)(2,1)} %shard_map.87), calls=%async_computation.1 | async-start | bytes 786432 | tf_op jit(solution)/shard_map/all_to_all | solution.py:230
  29.0 25.1 %copy-start.6 = (s32[16,6]{0,1:T(8,128)S(1)}, s32[16,6]{0,1:T(8,128)}, u32[]{:S(2)}) copy-start(s32[16,6]{0,1:T(8,128)} %param.9) | copy-start | bytes 1156
  29.0 32.1 %all-to-all-start = ((bf16[16,84,128]{2,1,0:T(8,128)(2,1)}), bf16[16,84,128]{2,1,0:T(8,128)(2,1)S(1)}, u32[]{:S(2)}, u32[]{:S(2)}) async-start(bf16[16,84,128]{2,1,0:T(8,128)(2,1)} %shard_map.86.rest_0_), calls=%async_computation | async-start | bytes 720896 | tf_op jit(solution)/shard_map/all_to_all | solution.py:230
  33.4 20.7 %collective-permute-start = (bf16[16,16,768]{2,1,0:T(8,128)(2,1)S(1)}, bf16[16,16,768]{2,1,0:T(8,128)(2,1)S(1)}, u32[]{:S(2)}, u32[]{:S(2)}) collective-permute-start(bf16[16,16,768]{2,1,0:T(8,128)(2,1)S(1)} %all-to-all-done.1.own.rest_0_), channel_id=1, source_target_pairs={{0,16},{16,0},{1,17},{17,1},{2,18},{18,2},{3,19},{19,3},{4,20},{20... | collective-permute-start | bytes 1179656 | tf_op jit(solution)/shard_map/ppermute | solution.py:256
  33.5 20.0 %collective-permute-start.1 = (bf16[16,84,128]{2,1,0:T(8,128)(2,1)}, bf16[16,84,128]{2,1,0:T(8,128)(2,1)S(1)}, u32[]{:S(2)}, u32[]{:S(2)}) collective-permute-start(bf16[16,84,128]{2,1,0:T(8,128)(2,1)} %shard_map.86.rest_0_), channel_id=1, source_target_pairs={{0,96},{32,0},{64,32},{96,64},{1,97},{33,1},{65,33},{97,65},{2,98}... | collective-permute-start | bytes 1032200 | tf_op jit(solution)/shard_map/ppermute | solution.py:255
  34.3 19.1 %collective-permute-start.2 = (bf16[16,84,128]{2,1,0:T(8,128)(2,1)}, bf16[16,84,128]{2,1,0:T(8,128)(2,1)S(1)}, u32[]{:S(2)}, u32[]{:S(2)}) collective-permute-start(bf16[16,84,128]{2,1,0:T(8,128)(2,1)} %shard_map.86.rest_0_), channel_id=1, source_target_pairs={{0,64},{32,96},{64,0},{96,32},{1,65},{33,97},{65,1},{97,33},{2,66}... | collective-permute-start | bytes 1032200 | tf_op jit(solution)/shard_map/ppermute | solution.py:255
  35.2 18.8 %collective-permute-start.3 = (bf16[16,84,128]{2,1,0:T(8,128)(2,1)}, bf16[16,84,128]{2,1,0:T(8,128)(2,1)S(1)}, u32[]{:S(2)}, u32[]{:S(2)}) collective-permute-start(bf16[16,84,128]{2,1,0:T(8,128)(2,1)} %shard_map.86.rest_0_), channel_id=1, source_target_pairs={{0,32},{32,64},{64,96},{96,0},{1,33},{33,65},{65,97},{97,1},{2,34}... | collective-permute-start | bytes 1032200 | tf_op jit(solution)/shard_map/ppermute | solution.py:255
  54.1 12.8 %copy-start.3 = (bf16[1,336,336]{2,1,0:T(8,128)(2,1)S(1)}, bf16[1,336,336]{2,1,0:T(8,128)(2,1)}, u32[]{:S(2)}) copy-start(bf16[1,336,336]{2,1,0:T(8,128)(2,1)} %param.11) | copy-start | bytes 677380
  56.7 6.7 %collective-permute-start.4 = (bf16[84,512]{1,0:T(8,128)(2,1)S(1)}, bf16[84,512]{1,0:T(8,128)(2,1)S(1)}, u32[]{:S(2)}, u32[]{:S(2)}) collective-permute-start(bf16[84,512]{1,0:T(8,128)(2,1)S(1)} %get-tuple-element.14), channel_id=1, source_target_pairs={{0,32},{32,64},{64,96},{96,0},{1,33},{33,65},{65,97},{97,1},{2,34}... | collective-permute-start | bytes 258056 | tf_op jit(solution)/shard_map/ppermute | solution.py:270
  59.4 6.7 %collective-permute-start.5 = (bf16[84,512]{1,0:T(8,128)(2,1)S(1)}, bf16[84,512]{1,0:T(8,128)(2,1)S(1)}, u32[]{:S(2)}, u32[]{:S(2)}) collective-permute-start(bf16[84,512]{1,0:T(8,128)(2,1)S(1)} %get-tuple-element.15), channel_id=1, source_target_pairs={{0,64},{32,96},{64,0},{96,32},{1,65},{33,97},{65,1},{97,33},{2,66}... | collective-permute-start | bytes 258056 | tf_op jit(solution)/shard_map/ppermute | solution.py:270
  59.5 7.4 %collective-permute-start.6 = (bf16[84,512]{1,0:T(8,128)(2,1)S(1)}, bf16[84,512]{1,0:T(8,128)(2,1)S(1)}, u32[]{:S(2)}, u32[]{:S(2)}) collective-permute-start(bf16[84,512]{1,0:T(8,128)(2,1)S(1)} %get-tuple-element.16), channel_id=1, source_target_pairs={{0,96},{32,0},{64,32},{96,64},{1,97},{33,1},{65,33},{97,65},{2,98}... | collective-permute-start | bytes 258056 | tf_op jit(solution)/shard_map/ppermute | solution.py:270
  68.4 9.6 %copy-start.1 = (bf16[16,84,128]{2,1,0:T(8,128)(2,1)}, bf16[16,84,128]{2,1,0:T(8,128)(2,1)S(1)}, u32[]{:S(2)}) copy-start(bf16[16,84,128]{2,1,0:T(8,128)(2,1)S(1)} %get-tuple-element.17.network) | copy-start | bytes 1032196
  68.4 28.0 %all-to-all-start.2 = ((bf16[16,172,128]{2,1,0:T(8,128)(2,1)}), bf16[16,172,128]{2,1,0:T(8,128)(2,1)S(1)}, u32[]{:S(2)}, u32[]{:S(2)}) async-start(bf16[16,172,128]{2,1,0:T(8,128)(2,1)} %get-tuple-element.18.sent), calls=%async_computation.2 | async-start | bytes 1441792 | tf_op jit(solution)/shard_map/all_to_all | solution.py:230
  79.7 6.2 %collective-permute-start.13 = (f32[4,48,128]{2,1,0:T(8,128)S(1)}, f32[4,48,128]{2,1,0:T(8,128)S(1)}, u32[]{:S(2)}, u32[]{:S(2)}) collective-permute-start(f32[4,48,128]{2,1,0:T(8,128)S(1)} %get-tuple-element.21), channel_id=1, source_target_pairs={{0,32},{32,64},{64,96},{96,0},{1,33},{33,65},{65,97},{97,1},{2,34}... | collective-permute-start | bytes 294920 | tf_op jit(solution)/shard_map/ppermute | solution.py:301
  80.5 25.6 %collective-permute-start.14 = (f32[4,48,128]{2,1,0:T(8,128)}, f32[4,48,128]{2,1,0:T(8,128)S(1)}, u32[]{:S(2)}, u32[]{:S(2)}) collective-permute-start(f32[4,48,128]{2,1,0:T(8,128)} %get-tuple-element.22), channel_id=1, source_target_pairs={{0,64},{32,96},{64,0},{96,32},{1,65},{33,97},{65,1},{97,33},{2,66}... | collective-permute-start | bytes 294920 | tf_op jit(solution)/shard_map/ppermute | solution.py:301
  80.8 25.3 %collective-permute-start.15 = (f32[4,48,128]{2,1,0:T(8,128)}, f32[4,48,128]{2,1,0:T(8,128)S(1)}, u32[]{:S(2)}, u32[]{:S(2)}) collective-permute-start(f32[4,48,128]{2,1,0:T(8,128)} %get-tuple-element.23), channel_id=1, source_target_pairs={{0,96},{32,0},{64,32},{96,64},{1,97},{33,1},{65,33},{97,65},{2,98}... | collective-permute-start | bytes 294920 | tf_op jit(solution)/shard_map/ppermute | solution.py:301
  81.9 27.0 %collective-permute-start.7 = (bf16[16,16,768]{2,1,0:T(8,128)(2,1)S(1)}, bf16[16,16,768]{2,1,0:T(8,128)(2,1)}, u32[]{:S(2)}, u32[]{:S(2)}) collective-permute-start(bf16[16,16,768]{2,1,0:T(8,128)(2,1)S(1)} %all-to-all-done.1.own.rest_0_), channel_id=1, source_target_pairs={{0,96},{32,0},{64,32},{96,64},{1,97},{33,1},{65,33},{97,65},{2,98}... | collective-permute-start | bytes 1179656 | tf_op jit(solution)/shard_map/ppermute | solution.py:280
  84.0 25.1 %collective-permute-start.8 = (bf16[16,16,768]{2,1,0:T(8,128)(2,1)S(1)}, bf16[16,16,768]{2,1,0:T(8,128)(2,1)}, u32[]{:S(2)}, u32[]{:S(2)}) collective-permute-start(bf16[16,16,768]{2,1,0:T(8,128)(2,1)S(1)} %all-to-all-done.1.own.rest_0_), channel_id=1, source_target_pairs={{0,64},{32,96},{64,0},{96,32},{1,65},{33,97},{65,1},{97,33},{2,66}... | collective-permute-start | bytes 1179656 | tf_op jit(solution)/shard_map/ppermute | solution.py:280
  85.9 23.6 %collective-permute-start.9 = (bf16[16,16,768]{2,1,0:T(8,128)(2,1)S(1)}, bf16[16,16,768]{2,1,0:T(8,128)(2,1)}, u32[]{:S(2)}, u32[]{:S(2)}) collective-permute-start(bf16[16,16,768]{2,1,0:T(8,128)(2,1)S(1)} %all-to-all-done.1.own.rest_0_), channel_id=1, source_target_pairs={{0,32},{32,64},{64,96},{96,0},{1,33},{33,65},{65,97},{97,1},{2,34}... | collective-permute-start | bytes 1179656 | tf_op jit(solution)/shard_map/ppermute | solution.py:280
  99.0 34.8 %all-to-all-start.3 = ((bf16[16,84,128]{2,1,0:T(8,128)(2,1)}), bf16[16,84,128]{2,1,0:T(8,128)(2,1)S(1)}, u32[]{:S(2)}, u32[]{:S(2)}) async-start(bf16[16,84,128]{2,1,0:T(8,128)(2,1)} %shard_map.91), calls=%async_computation.3 | async-start | bytes 720896 | tf_op jit(solution)/shard_map/all_to_all | solution.py:230
  106.2 10.3 %collective-permute-start.16 = (f32[48,128]{1,0:T(8,128)S(1)}, f32[48,128]{1,0:T(8,128)S(1)}, u32[]{:S(2)}, u32[]{:S(2)}) collective-permute-start(f32[48,128]{1,0:T(8,128)S(1)} %get-tuple-element.24), channel_id=1, source_target_pairs={{0,128},{128,0},{1,129},{129,1},{2,130},{130,2},{3,131},{131,3},{4... | collective-permute-start | bytes 73736 | tf_op jit(solution)/shard_map/ppermute | solution.py:305
  108.9 7.5 %collective-permute-start.17 = (f32[48,128]{1,0:T(8,128)S(1)}, f32[48,128]{1,0:T(8,128)S(1)}, u32[]{:S(2)}, u32[]{:S(2)}) collective-permute-start(f32[48,128]{1,0:T(8,128)S(1)} %get-tuple-element.26), channel_id=1, source_target_pairs={{0,144},{16,128},{128,16},{144,0},{1,145},{17,129},{129,17},{145,1... | collective-permute-start | bytes 73736 | tf_op jit(solution)/shard_map/ppermute | solution.py:306
  108.9 7.5 %collective-permute-start.18 = (f32[48,128]{1,0:T(8,128)S(1)}, f32[48,128]{1,0:T(8,128)S(1)}, u32[]{:S(2)}, u32[]{:S(2)}) collective-permute-start(f32[48,128]{1,0:T(8,128)S(1)} %get-tuple-element.25), channel_id=1, source_target_pairs={{0,16},{16,0},{1,17},{17,1},{2,18},{18,2},{3,19},{19,3},{4,20},{20... | collective-permute-start | bytes 73736 | tf_op jit(solution)/shard_map/ppermute | solution.py:307
  109.2 20.5 %collective-permute-start.10 = (bf16[16,16,768]{2,1,0:T(8,128)(2,1)}, bf16[16,16,768]{2,1,0:T(8,128)(2,1)S(1)}, u32[]{:S(2)}, u32[]{:S(2)}) collective-permute-start(bf16[16,16,768]{2,1,0:T(8,128)(2,1)} %collective-permute-done.7.rest_1_), channel_id=1, source_target_pairs={{0,16},{16,0},{1,17},{17,1},{2,18},{18,2},{3,19},{19,3},{4,20},{20... | collective-permute-start | bytes 1179656 | tf_op jit(solution)/shard_map/ppermute | solution.py:281
  109.5 20.2 %collective-permute-start.11 = (bf16[16,16,768]{2,1,0:T(8,128)(2,1)}, bf16[16,16,768]{2,1,0:T(8,128)(2,1)S(1)}, u32[]{:S(2)}, u32[]{:S(2)}) collective-permute-start(bf16[16,16,768]{2,1,0:T(8,128)(2,1)} %collective-permute-done.8.rest_2_), channel_id=1, source_target_pairs={{0,16},{16,0},{1,17},{17,1},{2,18},{18,2},{3,19},{19,3},{4,20},{20... | collective-permute-start | bytes 1179656 | tf_op jit(solution)/shard_map/ppermute | solution.py:281
  116.5 13.2 %collective-permute-start.12 = (bf16[16,16,768]{2,1,0:T(8,128)(2,1)}, bf16[16,16,768]{2,1,0:T(8,128)(2,1)S(1)}, u32[]{:S(2)}, u32[]{:S(2)}) collective-permute-start(bf16[16,16,768]{2,1,0:T(8,128)(2,1)} %collective-permute-done.9.rest_3_), channel_id=1, source_target_pairs={{0,16},{16,0},{1,17},{17,1},{2,18},{18,2},{3,19},{19,3},{4,20},{20... | collective-permute-start | bytes 1179656 | tf_op jit(solution)/shard_map/ppermute | solution.py:281
  116.5 11.1 %collective-permute-start.19 = (f32[24,128]{1,0:T(8,128)S(1)}, f32[24,128]{1,0:T(8,128)S(1)}, u32[]{:S(2)}, u32[]{:S(2)}) collective-permute-start(f32[24,128]{1,0:T(8,128)S(1)} %get-tuple-element.27), channel_id=1, source_target_pairs={{0,0},{1,16},{2,32},{3,48},{4,64},{5,80},{6,96},{7,112},{8,128},{9... | collective-permute-start | bytes 36872 | tf_op jit(solution)/shard_map/ppermute | solution.py:310
  127.6 0.7 copy-start.8
  128.3 1.3 copy-start.7
  129.6 1.0 copy-start.2
